TPU v7x, 32 devices: a whole 2x2x4 slice. The times are simulated.
32 devices in a mesh: mode: 4 (over z), samp: 4 (over x, core), pts: 2 (over y).
Axes of the slice: x: 2, y: 2, z: 4, core: 2. Of those that a mesh axis runs over, the one named last changes fastest.
Arguments:
- coefficients: bfloat16 [768, 12288], P('samp', 'mode'), may hold values from -15 to 15
- panels: bfloat16 [12288, 16384], P(('mode', 'samp'), 'pts'), may hold values from -0.02734375 to 0.02734375
- mean_field: float32 [16384], P('pts'), may hold values from -3 to 3
- load: float32 [16384], P('pts'), may hold values from 0.5 to 2
Outputs:
- standardized: float32 [768], P('samp')
All inputs are finite; a program needn't handle non-finite values.
Results may differ from a plain program's by a relative error of at most 0.0003.
Values may be sent and summed in bfloat16 or wider, within the bound.
A program may use at most 128 MiB of HBM per device.

v0:
```python
import jax
import jax.numpy as jnp
from jax import lax
from jax.sharding import PartitionSpec as P

POINTS = 16384


def point_sums(weighted):
    fine_part = jnp.sum(weighted, axis=1) / POINTS
    coarse_part = jnp.sum(weighted[:, ::2], axis=1) * (2.0 / POINTS)
    return (fine_part, coarse_part)


def body(coefficients, panels, mean_field, load):
    samples = coefficients.shape[0]
    partial_value = jnp.dot(
        coefficients,
        lax.all_gather(panels, "samp", axis=0, tiled=True),
        preferred_element_type=jnp.float32,
    )
    portion = lax.psum_scatter(partial_value, "mode", scatter_dimension=1, tiled=True)
    count = portion.shape[1]
    offset = lax.axis_index("mode") * count
    local_mean = lax.dynamic_slice_in_dim(mean_field, offset, count, 0)
    local_load = lax.dynamic_slice_in_dim(load, offset, count, 0)
    weighted = local_load[None, :] * jnp.exp(portion + local_mean[None, :])
    fine_part, coarse_part = point_sums(weighted)
    fine_qoi, coarse_qoi = lax.psum((fine_part, coarse_part), ("mode", "pts"))
    level_diff = fine_qoi - coarse_qoi
    total_samples = samples * lax.axis_size("samp")
    center = lax.psum(jnp.sum(level_diff), "samp") / total_samples
    shifted = level_diff - center
    spread = lax.psum(jnp.sum(shifted * shifted), "samp") / total_samples
    return shifted / jnp.sqrt(spread + 1e-06)


def solution(mesh):
    in_specs = (P("samp", "mode"), P(("mode", "samp"), "pts"), P("pts"), P("pts"))
    out_specs = P("samp")
    return jax.shard_map(body, mesh=mesh, in_specs=in_specs, out_specs=out_specs, check_vma=False)
```

profile of v0, /device:TPU:0, one launch (start us, length us, event | category | flops | bytes accessed | tf_op | source)
XLA Modules:
  0.0 513.9 jit_solution(14702071520744668993)
XLA Ops:
  6.5 0.0 copy-start
  6.5 0.0 all-gather.2.cloned.1.call-start
  6.5 0.7 all-gather.2.cloned.1.call-update
  7.3 0.0 reduce-scatter.2.cloned.1.call-start
  7.3 301.5 %all-gather.2.cloned.1.call-done = bf16[3072,8192]{1,0:T(8,128)(2,1)} async-done(((bf16[768,8192]{1,0:T(8,128)(2,1)}), bf16[3072,8192]{1,0:T(8,128)(2,1)}) %all-gather.2.cloned.1.call-update) | async-done | bytes 50331664 | tf_op jit(solution)/shard_map/all_gather | solution.py:19
  308.8 0.0 copy-done
  308.8 21.6 %fusion.2 = f32[192,8192]{1,0:T(8,128)} fusion(bf16[192,3072]{1,0:T(8,128)(2,1)S(1)} %copy-done, bf16[3072,8192]{1,0:T(8,128)(2,1)} %all-gather.2.cloned.1.call-done), kind=kOutput, calls=%fused_computation.7 | convolution fusion | flops 9663676416 | bytes 57802752 | tf_op jit(solution)/shard_map/dot_general | solution.py:17
  330.4 0.0 reduce-scatter.2.cloned.1.call-update
  330.4 0.7 dynamic_slice.7
  331.1 0.7 dynamic_slice.6
  331.8 109.5 %reduce-scatter.2.cloned.1.call-done = f32[192,2048]{1,0:T(8,128)} async-done(((f32[192,8192]{1,0:T(8,128)}), f32[192,2048]{1,0:T(8,128)}) %reduce-scatter.2.cloned.1.call-update) | async-done | bytes 1572880 | tf_op jit(solution)/shard_map/reduce_scatter | solution.py:22
  441.3 0.0 copy-start.1
  441.3 1.9 fusion.1
  443.2 26.3 %slice.3 = f32[192,1024]{1,0:T(8,128)S(1)} slice(f32[192,2048]{1,0:T(8,128)S(1)} %get-tuple-element.10), slice={[0:192:1], [0:2048:2]} | slice | bytes 1572864 | tf_op jit(solution)/shard_map/slice | solution.py:11
  469.5 0.1 reduce_sum.37
  469.7 20.9 %all-reduce = (f32[192]{0:T(256)S(1)}, f32[192]{0:T(256)S(1)}) all-reduce(f32[192]{0:T(256)S(1)} %get-tuple-element.12, f32[192]{0:T(256)S(1)} %get-tuple-element.11), channel_id=1, replica_groups=mesh['mode'=4,'samp'=4,'pts'=2] {'mode','pts'}, use_global_device_ids=true, to_apply=%region_2.0 | all-reduce | flops 384 | bytes 3072 | tf_op jit(solution)/shard_map/psum | solution.py:29
  490.5 0.6 fusion
  491.1 6.3 %psum.30 = f32[]{:T(128)} all-reduce(f32[]{:T(128)} %get-tuple-element.7), channel_id=1, replica_groups=mesh['mode'=4,'samp'=4,'pts'=2] {'samp'}, use_global_device_ids=true, to_apply=%region_6.0 | all-reduce | flops 1 | bytes 8 | tf_op jit(solution)/shard_map/psum | solution.py:32
  498.0 0.6 multiply_reduce_fusion
  498.6 7.2 %psum.31 = f32[]{:T(128)} all-reduce(f32[]{:T(128)} %multiply_reduce_fusion), channel_id=1, replica_groups=mesh['mode'=4,'samp'=4,'pts'=2] {'samp'}, use_global_device_ids=true, to_apply=%region_8.0 | all-reduce | flops 1 | bytes 8 | tf_op jit(solution)/shard_map/psum | solution.py:34
  506.5 0.6 subtract_divide_fusion
  507.1 0.0 copy-done.1
  (1 shorter events, 0.0 us)
Async XLA Ops:
  6.5 302.2 %copy-start = (bf16[192,3072]{1,0:T(8,128)(2,1)S(1)}, bf16[192,3072]{1,0:T(8,128)(2,1)}, u32[]{:S(2)}) copy-start(bf16[192,3072]{1,0:T(8,128)(2,1)} %param.4) | copy-start | bytes 3538948
  6.5 302.2 %all-gather.2.cloned.1.call-start = ((), (), s32[]{:S(2)}) async-start(), calls=%async_computation.1 | async-start | bytes 62914560 | tf_op jit(solution)/shard_map/all_gather | solution.py:19
  7.3 434.1 %reduce-scatter.2.cloned.1.call-start = ((), (), s32[]{:S(2)}) async-start(), calls=%async_computation.2 | async-start | bytes 7864320 | tf_op jit(solution)/shard_map/reduce_scatter | solution.py:22
  441.3 65.8 %copy-start.1 = (bf16[192,3072]{1,0:T(8,128)(2,1)S(1)}, bf16[192,3072]{1,0:T(8,128)(2,1)}, u32[]{:S(2)}) copy-start(bf16[192,3072]{1,0:T(8,128)(2,1)} %param.4) | copy-start | bytes 3538948
Sparse Core Ops, SparseCore 0:
  8.9 299.8 all-gather.1
  330.5 110.7 reduce-scatter.1
where the time goes:
time: 514 us
  waiting for transfers between devices  412 us (80%)
  blocking collectives  34.3 us (7%)
  local copies, waits for them, and re-layouts  27.7 us (5%)
  matrix products  21.6 us (4%)
  between operations  14.8 us (3%)
    all_gather x1, waiting for transfers between devices, body(): lax.all_gather(panels, 'samp', axis=0, tiled=True)  301 us
    reduce_scatter x1, waiting for transfers between devices, body(): lax.psum_scatter(partial_value, 'mode', scatter_dimension=1, tiled=True)  110 us
    slice x1, local copies, waits for them, and re-layouts, point_sums(): coarse_part = jnp.sum(weighted[:, ::2], axis=1) * (2.0 / POINTS)  26.3 us
    dot_general x1, matrix products, body(): jnp.dot(coefficients, lax.all_gather(panels, 'samp', axis=0, tiled=True),...  21.6 us
    psum x1, blocking collectives, body(): fine_qoi, coarse_qoi = lax.psum((fine_part, coarse_part), ('mode', 'pts'))  20.9 us
  transfers between devices with their start and end apart: 2, of which 2 were waited for; matrix products, arithmetic and copies ran while one was open for 0% of the time, Pallas kernels for 0%

commit v1 on v0

v1 whole, which is shorter than its diff:
```python
import jax
import jax.numpy as jnp
from jax import lax
from jax.sharding import PartitionSpec as P


def body(points, coefficients, panels, mean_field, load):
    rows = lax.all_gather(coefficients, "samp", axis=0, tiled=True)
    mine = lax.all_to_all(panels, "samp", split_axis=1, concat_axis=0, tiled=True)
    partial_value = jnp.dot(rows, mine, preferred_element_type=jnp.float32)
    portion = lax.psum_scatter(partial_value, "mode", scatter_dimension=1, tiled=True)
    count = portion.shape[1]
    offset = lax.axis_index("samp") * mine.shape[1] + lax.axis_index("mode") * count
    local_mean = lax.dynamic_slice_in_dim(mean_field, offset, count, 0)
    local_load = lax.dynamic_slice_in_dim(load, offset, count, 0)
    weighted = local_load[None, :] * jnp.exp(portion + local_mean[None, :])
    even = (lax.broadcasted_iota(jnp.int32, (1, count), 1) % 2) == 0
    fine = jnp.sum(weighted, axis=1)
    coarse = jnp.sum(jnp.where(even, weighted, 0.0), axis=1)
    fine, coarse = lax.psum((fine, coarse), ("mode", "samp", "pts"))
    level_diff = fine / points - coarse * (2.0 / points)
    total = level_diff.shape[0]
    center = jnp.sum(level_diff) / total
    shifted = level_diff - center
    spread = jnp.sum(shifted * shifted) / total
    out = shifted / jnp.sqrt(spread + 1e-06)
    own = coefficients.shape[0]
    return lax.dynamic_slice_in_dim(out, lax.axis_index("samp") * own, own, 0)


def solution(mesh):
    in_specs = (P("samp", "mode"), P(("mode", "samp"), "pts"), P("pts"), P("pts"))

    def run(coefficients, panels, mean_field, load):
        def inner(*args):
            return body(mean_field.shape[0], *args)

        return jax.shard_map(inner, mesh=mesh, in_specs=in_specs, out_specs=P("samp"), check_vma=False)(
            coefficients, panels, mean_field, load
        )

    return run
```

time: 514 us -> 391 us (0.76)
  waiting for transfers between devices: 412 us -> 274 us
  local copies, waits for them, and re-layouts: 27.7 us -> 34.6 us
  blocking collectives: 34.3 us -> 40.8 us
  starting transfers between devices: 0.04 us -> 6.41 us
  matrix products: 21.6 us -> 15.9 us
    all_gather x1, waiting for transfers between devices: 301 us -> 0.01 us  [body(): rows = lax.all_gather(coefficients, 'samp', axis=0, tiled=True)]
    all_to_all x0 -> x1, waiting for transfers between devices: none -> 163 us  [body(): lax.all_to_all(panels, 'samp', split_axis=1, concat_axis=0, tiled=True)]
    slice x1 -> x0, local copies, waits for them, and re-layouts: 26.3 us -> none  [point_sums(): coarse_part = jnp.sum(weighted[:, ::2], axis=1) * (2.0 / POINTS)]
    unnamed x4 -> x1, local copies, waits for them, and re-layouts: 0.01 us -> 16.6 us
    all_to_all x0 -> x1, local copies, waits for them, and re-layouts: none -> 15.8 us  [body(): lax.all_to_all(panels, 'samp', split_axis=1, concat_axis=0, tiled=True)]
    psum x3 -> x1, blocking collectives: 34.3 us -> 40.8 us  [body(): fine, coarse = lax.psum((fine, coarse), ('mode', 'samp', 'pts'))]
    all_to_all x0 -> x1, starting transfers between devices: none -> 6.33 us  [body(): lax.all_to_all(panels, 'samp', split_axis=1, concat_axis=0, tiled=True)]
    dot_general x1, matrix products: 21.6 us -> 15.9 us  [body(): partial_value = jnp.dot(rows, mine, preferred_element_type=jnp.float32)]
  transfers between devices with their start and end apart: 2 -> 3, of which waited for: 2 -> 2; matrix products, arithmetic and copies ran while one was open for 0% -> 4% of each run, Pallas kernels for 0% -> 0%
where the time goes in v1:
time: 391 us; the launch traced here: 390 us
  waiting for transfers between devices  274 us (70%)
  blocking collectives  40.8 us (10%)
  local copies, waits for them, and re-layouts  34.6 us (9%)
  matrix products  15.9 us (4%)
  between operations  14.8 us (4%)
  starting transfers between devices  6.41 us (2%)
    all_to_all x1, waiting for transfers between devices, body(): lax.all_to_all(panels, 'samp', split_axis=1, concat_axis=0, tiled=True)  163 us
    reduce_scatter x1, waiting for transfers between devices, body(): lax.psum_scatter(partial_value, 'mode', scatter_dimension=1, tiled=True)  111 us
    psum x1, blocking collectives, body(): fine, coarse = lax.psum((fine, coarse), ('mode', 'samp', 'pts'))  40.8 us
    unnamed x1, local copies, waits for them, and re-layouts  16.6 us
    dot_general x1, matrix products, body(): partial_value = jnp.dot(rows, mine, preferred_element_type=jnp.float32)  15.9 us
    all_to_all x1, local copies, waits for them, and re-layouts, body(): lax.all_to_all(panels, 'samp', split_axis=1, concat_axis=0, tiled=True)  15.8 us
  transfers between devices with their start and end apart: 3, of which 2 were waited for; matrix products, arithmetic and copies ran while one was open for 4% of the time, Pallas kernels for 0%

profile of v1, /device:TPU:0, one launch (start us, length us, event | category | flops | bytes accessed | tf_op | source)
XLA Modules:
  0.0 390.0 jit_solution(15918582393272994374)
XLA Ops:
  6.5 16.6 %copy.5 = bf16[768,8192]{0,1:T(8,128)(2,1)} copy(bf16[768,8192]{1,0:T(8,128)(2,1)} %param.5) | data formatting | bytes 25165824 | tf_op args[1]
  23.2 6.3 %all-to-all-start = ((bf16[768,4,2048]{0,2,1:T(8,128)(2,1)}), bf16[768,4,2048]{0,2,1:T(8,128)(2,1)}, u32[]{:S(2)}, u32[]{:S(2)}) async-start(bf16[768,4,2048]{0,2,1:T(8,128)(2,1)} %bitcast.5), calls=%async_computation | async-start | bytes 25165824 | tf_op jit(solution)/shard_map/all_to_all | solution.py:9
  29.5 0.0 all-gather.2.cloned.1.call-start
  29.6 0.7 all-gather.2.cloned.1.call-update
  30.2 0.0 reduce-scatter.2.cloned.1.call-start
  30.3 163.2 %all-to-all-done = bf16[768,4,2048]{0,2,1:T(8,128)(2,1)} async-done(((bf16[768,4,2048]{0,2,1:T(8,128)(2,1)}), bf16[768,4,2048]{0,2,1:T(8,128)(2,1)}, u32[]{:S(2)}, u32[]{:S(2)}) %all-to-all-start) | async-done | bytes 12582944 | tf_op jit(solution)/shard_map/all_to_all | solution.py:9
  193.5 15.8 %copy.6 = bf16[4,768,2048]{2,1,0:T(8,128)(2,1)} copy(bf16[4,768,2048]{1,2,0:T(8,128)(2,1)} %bitcast.1) | data formatting | bytes 25165824 | tf_op jit(solution)/shard_map/all_to_all | solution.py:9
  209.3 0.0 all-gather.2.cloned.1.call-done
  209.3 15.9 %fusion.6 = f32[768,2048]{1,0:T(8,128)} fusion(bf16[768,3072]{1,0:T(8,128)(2,1)} %all-gather.2.cloned.1.call-done, bf16[3072,2048]{1,0:T(8,128)(2,1)} %bitcast.6), kind=kOutput, calls=%fused_computation.13 | convolution fusion | flops 9663676416 | bytes 23592960 | tf_op jit(solution)/shard_map/dot_general | solution.py:10
  225.1 0.0 reduce-scatter.2.cloned.1.call-update
  225.2 0.8 dynamic_slice.10
  225.9 0.8 dynamic_slice.9
  226.7 110.6 %reduce-scatter.2.cloned.1.call-done = f32[768,512]{1,0:T(8,128)} async-done(((f32[768,2048]{1,0:T(8,128)}), f32[768,512]{1,0:T(8,128)}) %reduce-scatter.2.cloned.1.call-update) | async-done | bytes 1572880 | tf_op jit(solution)/shard_map/reduce_scatter | solution.py:11
  337.3 1.8 fusion
  339.1 40.8 %all-reduce = (f32[768]{0:T(1024)S(1)}, f32[768]{0:T(1024)S(1)}) all-reduce(f32[768]{0:T(1024)S(1)} %get-tuple-element.6, f32[768]{0:T(1024)S(1)} %get-tuple-element.5), channel_id=1, replica_groups=mesh['mode'=4,'samp'=4,'pts'=2] {'mode','samp','pts'}, use_global_device_ids=true, to_apply=%region_4.5 | all-reduce | flops 1536 | bytes 12288 | tf_op jit(solution)/shard_map/psum | solution.py:20
  379.9 0.6 fusion.5
  381.2 0.6 multiply_reduce_fusion
  382.5 0.6 dynamic_slice.11
  (2 shorter events, 0.0 us)
Async XLA Ops:
  23.2 170.3 %all-to-all-start = ((bf16[768,4,2048]{0,2,1:T(8,128)(2,1)}), bf16[768,4,2048]{0,2,1:T(8,128)(2,1)}, u32[]{:S(2)}, u32[]{:S(2)}) async-start(bf16[768,4,2048]{0,2,1:T(8,128)(2,1)} %bitcast.5), calls=%async_computation | async-start | bytes 25165824 | tf_op jit(solution)/shard_map/all_to_all | solution.py:9
  29.5 179.7 %all-gather.2.cloned.1.call-start = ((), (), s32[]{:S(2)}) async-start(), calls=%async_computation.2 | async-start | bytes 5898240 | tf_op jit(solution)/shard_map/all_gather | solution.py:8
  30.2 307.0 %reduce-scatter.2.cloned.1.call-start = ((), (), s32[]{:S(2)}) async-start(), calls=%async_computation.3 | async-start | bytes 7864320 | tf_op jit(solution)/shard_map/reduce_scatter | solution.py:11
Sparse Core Ops, SparseCore 0:
  31.9 65.9 all-gather.1
  225.3 111.9 reduce-scatter.1

commit v2 on v1

--- a/solution.py
+++ b/solution.py
@@ -1,10 +1,233 @@
+import functools
+
 import jax
 import jax.numpy as jnp
 from jax import lax
+from jax.experimental import pallas as pl
+from jax.experimental.pallas import tpu as pltpu
 from jax.sharding import PartitionSpec as P
 
-
-def body(points, coefficients, panels, mean_field, load):
+MESH = pl.DeviceIdType.MESH
+WIDTH = 256
+LANES = 128
+
+
+def kernel(
+    depth, chunks, coef_hbm, panel_hbm, mean_ref, load_ref, acc_ref,
+    coef, panel, out, core_in, cross_in, line_in_x, line_in_z,
+    coef_send, coef_recv, coef_local, panel_sem,
+    core_send, core_recv, cross_send, cross_recv, line_send, line_recv,
+):
+    samp, line = lax.axis_index("samp"), lax.axis_index("mode")
+    length = lax.axis_size("mode")
+    last = length - 1
+    rows = coef_hbm.shape[0]
+    partner = samp + 1 - 2 * lax.rem(samp, 2)
+    across = lax.rem(samp + 2, 4)
+    diagonal = lax.rem(partner + 2, 4)
+    peers = (across, partner, diagonal)
+
+    barrier = pltpu.get_barrier_semaphore()
+    for peer in peers:
+        pl.semaphore_signal(barrier, inc=1, device_id={"samp": peer}, device_id_type=MESH)
+    for peer in (lax.rem(line + 1, length), lax.rem(line + last, length)):
+        pl.semaphore_signal(barrier, inc=1, device_id={"mode": peer}, device_id_type=MESH)
+    pl.semaphore_wait(barrier, 5)
+
+    def panel_copy(j):
+        slot = lax.rem(j, 2)
+        columns = pl.ds(pl.multiple_of(j * WIDTH, WIDTH), WIDTH)
+        return pltpu.make_async_copy(panel_hbm.at[:, columns], panel.at[slot], panel_sem.at[slot])
+
+    def coef_copy(i):
+        columns = pl.ds(pl.multiple_of(peers[i] * depth, depth), depth)
+        return pltpu.make_async_remote_copy(
+            coef_hbm.at[:, columns], coef.at[pl.ds((i + 1) * rows, rows), :],
+            coef_send.at[i], coef_recv.at[i], device_id={"samp": peers[i]}, device_id_type=MESH,
+        )
+
+    for i in (0, 2, 1):
+        coef_copy(i).start()
+    own = pltpu.make_async_copy(
+        coef_hbm.at[:, pl.ds(pl.multiple_of(samp * depth, depth), depth)], coef.at[pl.ds(0, rows), :], coef_local
+    )
+    own.start()
+    panel_copy(0).start()
+    acc_ref[...] = jnp.zeros_like(acc_ref)
+
+    def core_copy(j):
+        return pltpu.make_async_remote_copy(
+            out.at[j, pl.ds(2 * rows, 2 * rows), :], core_in.at[j],
+            core_send.at[j], core_recv.at[j], device_id={"samp": partner}, device_id_type=MESH,
+        )
+
+    def cross_copy(j):
+        return pltpu.make_async_remote_copy(
+            out.at[j, pl.ds(rows, rows), :], cross_in.at[j],
+            cross_send.at[j], cross_recv.at[j], device_id={"samp": across}, device_id_type=MESH,
+        )
+
+    def up(j):
+        return lax.rem(j // 2, 2)
+
+    def place(j):
+        return up(j) * line + (1 - up(j)) * (last - line)
+
+    def line_copy(j, kind):
+        size = (1 + kind) * rows
+        into = line_in_z if kind else line_in_x
+        target = lax.rem(line + 2 * up(j) - 1 + length, length)
+        return pltpu.make_async_remote_copy(
+            out.at[j, pl.ds(0, size), :], into.at[j // 2],
+            line_send.at[j], line_recv.at[j], device_id={"mode": target}, device_id_type=MESH,
+        )
+
+    def finish(j, field):
+        columns = pl.ds(pl.multiple_of(j * WIDTH, WIDTH), WIDTH)
+        weighted = load_ref[:, columns] * jnp.exp(field + mean_ref[:, columns])
+        total = acc_ref[...]
+        for at in range(0, WIDTH, LANES):
+            total = total + weighted[:, at : at + LANES]
+        acc_ref[...] = total
+
+    def begin(j):
+        @pl.when(j + 1 < chunks)
+        def _():
+            panel_copy(j + 1).start()
+
+        panel_copy(j).wait()
+        out[j] = jnp.dot(coef[...], panel[lax.rem(j, 2)], preferred_element_type=jnp.float32)
+        core_copy(j).start()
+
+    def joined(j):
+        core_copy(j).wait_recv()
+        out[j, pl.ds(0, 2 * rows), :] += core_in[j]
+
+        @pl.when(lax.rem(j, 2) == 0)
+        def _():
+            cross_copy(j).start()
+
+        @pl.when((lax.rem(j, 2) == 1) & (place(j) == 0))
+        def _():
+            line_copy(j, 1).start()
+
+    def crossed(j):
+        cross_copy(j).wait_recv()
+        out[j, pl.ds(0, rows), :] += cross_in[j]
+
+        @pl.when(place(j) == 0)
+        def _():
+            line_copy(j, 0).start()
+
+    def hop(j, kind, at):
+        @pl.when(place(j) == at)
+        def _():
+            line_copy(j, kind).wait_recv()
+            if at < last:
+                out[j, pl.ds(0, (1 + kind) * rows), :] += (line_in_z if kind else line_in_x)[j // 2]
+                line_copy(j, kind).start()
+            elif kind:
+                out[j, pl.ds(0, 2 * rows), :] += line_in_z[j // 2]
+                cross_copy(j).start()
+            else:
+                finish(j, out[j, pl.ds(0, rows), :] + line_in_x[j // 2])
+
+    def back(j):
+        @pl.when(place(j) == last)
+        def _():
+            cross_copy(j).wait_recv()
+            finish(j, out[j, pl.ds(0, rows), :] + cross_in[j])
+
+    own.wait()
+    for i in range(3):
+        coef_copy(i).wait()
+
+    stages = [(0, None, begin), (1, None, joined), (1 + CROSS_LAG, 0, crossed)]
+    for at in range(1, last + 1):
+        stages.append((1 + CROSS_LAG + LINE_LAG * at, 0, functools.partial(hop, kind=0, at=at)))
+        stages.append((1 + WIDE_LAG * at, 1, functools.partial(hop, kind=1, at=at)))
+    stages.append((1 + WIDE_LAG * last + CROSS_LAG, 1, back))
+    end = max(lag for lag, _, _ in stages)
+
+    def tick(t, carry):
+        for lag, kind, stage in stages:
+            j = t - lag
+            here = (j >= 0) & (j < chunks)
+            if kind is not None:
+                here = here & (lax.rem(j + 2 * end, 2) == kind)
+            pl.when(here)(functools.partial(stage, j))
+        return carry
+
+    lax.fori_loop(0, chunks + end, tick, 0)
+
+    def drain(j, carry):
+        core_copy(j).wait_send()
+        even, final = lax.rem(j, 2) == 0, place(j) == last
+
+        @pl.when(even | final)
+        def _():
+            cross_copy(j).wait_send()
+
+        @pl.when(even & (place(j) < last))
+        def _():
+            line_copy(j, 0).wait_send()
+
+        @pl.when((lax.rem(j, 2) == 1) & (place(j) < last))
+        def _():
+            line_copy(j, 1).wait_send()
+
+        return carry
+
+    lax.fori_loop(0, chunks, drain, 0)
+
+
+CROSS_LAG, LINE_LAG, WIDE_LAG = 3, 2, 4
+
+
+def lane_sums(coefficients, panels, mean_field, load):
+    rows = coefficients.shape[0]
+    depth, points = panels.shape
+    chunks = points // WIDTH
+    every = pl.BlockSpec(memory_space=pl.ANY)
+    here = pl.BlockSpec(memory_space=pltpu.VMEM)
+    dma = pltpu.SemaphoreType.DMA
+    f32 = jnp.float32
+    return pl.pallas_call(
+        functools.partial(kernel, depth, chunks),
+        out_shape=jax.ShapeDtypeStruct((rows, LANES), f32),
+        in_specs=[every, every, here, here],
+        out_specs=here,
+        scratch_shapes=[
+            pltpu.VMEM((4 * rows, depth), jnp.bfloat16),
+            pltpu.VMEM((2, depth, WIDTH), jnp.bfloat16),
+            pltpu.VMEM((chunks, 4 * rows, WIDTH), f32),
+            pltpu.VMEM((chunks, 2 * rows, WIDTH), f32),
+            pltpu.VMEM((chunks, rows, WIDTH), f32),
+            pltpu.VMEM((chunks // 2, rows, WIDTH), f32),
+            pltpu.VMEM((chunks // 2, 2 * rows, WIDTH), f32),
+            dma((3,)), dma((3,)), dma, dma((2,)),
+            dma((chunks,)), dma((chunks,)), dma((chunks,)), dma((chunks,)), dma((chunks,)), dma((chunks,)),
+        ],
+        compiler_params=pltpu.CompilerParams(
+            collective_id=0, has_side_effects=True, vmem_limit_bytes=67043328
+        ),
+    )(coefficients, panels, mean_field[None, :], load[None, :])
+
+
+def lined(points, coefficients, panels, mean_field, load):
+    sums = lane_sums(coefficients, panels, mean_field, load)
+    even = (lax.broadcasted_iota(jnp.int32, (1, LANES), 1) % 2) == 0
+    parts = jnp.sum(sums, axis=1), jnp.sum(jnp.where(even, sums, 0.0), axis=1)
+    fine, coarse = lax.psum(parts, ("mode", "pts"))
+    level_diff = fine / points - coarse * (2.0 / points)
+    total = level_diff.shape[0] * lax.axis_size("samp")
+    center = lax.psum(jnp.sum(level_diff), "samp") / total
+    shifted = level_diff - center
+    spread = lax.psum(jnp.sum(shifted * shifted), "samp") / total
+    return shifted / jnp.sqrt(spread + 1e-06)
+
+
+def gathered(points, coefficients, panels, mean_field, load):
     rows = lax.all_gather(coefficients, "samp", axis=0, tiled=True)
     mine = lax.all_to_all(panels, "samp", split_axis=1, concat_axis=0, tiled=True)
     partial_value = jnp.dot(rows, mine, preferred_element_type=jnp.float32)
@@ -33,7 +256,8 @@
 
     def run(coefficients, panels, mean_field, load):
         def inner(*args):
-            return body(mean_field.shape[0], *args)
+            form = lined if mesh.shape["samp"] == 4 and mesh.shape["mode"] > 2 else gathered
+            return form(mean_field.shape[0], *args)
 
         return jax.shard_map(inner, mesh=mesh, in_specs=in_specs, out_specs=P("samp"), check_vma=False)(
             coefficients, panels, mean_field, load

time: 391 us -> 204 us (0.52)
  waiting for transfers between devices: 274 us -> 0 us
  Pallas kernels: 0 us -> 160 us
  local copies, waits for them, and re-layouts: 34.6 us -> 0 us
  matrix products: 15.9 us -> 0 us
  between operations: 14.8 us -> 1.36 us
  starting transfers between devices: 6.41 us -> 0 us
    all_to_all x1 -> x0, waiting for transfers between devices: 163 us -> none  [body(): lax.all_to_all(panels, 'samp', split_axis=1, concat_axis=0, tiled=True)]
    pallas_call x0 -> x1, Pallas kernels: none -> 160 us  [lane_sums(): pl.pallas_call(functools.partial(kernel, depth, chunks), out_shape=jax.Sh...]
    reduce_scatter x1 -> x0, waiting for transfers between devices: 111 us -> none  [body(): lax.psum_scatter(partial_value, 'mode', scatter_dimension=1, tiled=True)]
    unnamed x1 -> x0, local copies, waits for them, and re-layouts: 16.6 us -> none
    dot_general x1 -> x0, matrix products: 15.9 us -> none  [body(): partial_value = jnp.dot(rows, mine, preferred_element_type=jnp.float32)]
    all_to_all x1 -> x0, local copies, waits for them, and re-layouts: 15.8 us -> none  [body(): lax.all_to_all(panels, 'samp', split_axis=1, concat_axis=0, tiled=True)]
    all_to_all x1 -> x0, starting transfers between devices: 6.33 us -> none  [body(): lax.all_to_all(panels, 'samp', split_axis=1, concat_axis=0, tiled=True)]
    psum x1 -> x3, blocking collectives: 40.8 us -> 38.4 us  [the longest x1 25.2 us: lined(): fine, coarse = lax.psum(parts, ('mode', 'pts'))]
  transfers between devices with their start and end apart: 3 -> 0, of which waited for: 2 -> 0; matrix products, arithmetic and copies ran while one was open for 4% -> 0% of each run, Pallas kernels for 0% -> 0%
where the time goes in v2:
time: 204 us; the launch traced here: 203 us
  Pallas kernels  160 us (78%)
  blocking collectives  38.4 us (19%)
  other arithmetic  3.34 us (2%)
    pallas_call x1, Pallas kernels, lane_sums(): pl.pallas_call(functools.partial(kernel, depth, chunks), out_shape=jax.Sh...  160 us
    psum x1, blocking collectives, lined(): fine, coarse = lax.psum(parts, ('mode', 'pts'))  25.2 us
    psum x1, blocking collectives, lined(): spread = lax.psum(jnp.sum(shifted * shifted), 'samp') / total  7 us
    psum x1, blocking collectives, lined(): center = lax.psum(jnp.sum(level_diff), 'samp') / total  6.27 us

profile of v2, /device:TPU:0, one launch (start us, length us, event | category | flops | bytes accessed | tf_op | source)
XLA Modules:
  0.0 203.0 jit_solution(2604695401639485823)
XLA Ops:
  0.0 0.5 fusion
  0.5 159.9 %shard_map.46 = f32[192,128]{1,0:T(8,128)} custom-call(bf16[192,3072]{1,0:T(8,128)(2,1)} %coef_hbm.1, bf16[768,8192]{1,0:T(8,128)(2,1)} %panel_hbm.1, f32[1,8192]{1,0:T(1,128)} %bitcast.2, f32[1,8192]{1,0:T(1,128)} %bitcast.3), custom_call_target="tpu_custom_call" | custom-call | tf_op jit(solution)/shard_map/pallas_call | solution.py:195
  160.4 1.0 fusion.2
  161.4 25.2 %all-reduce = (f32[192]{0:T(256)S(1)}, f32[192]{0:T(256)S(1)}) all-reduce(f32[192]{0:T(256)S(1)} %get-tuple-element.6, f32[192]{0:T(256)S(1)} %get-tuple-element.5), channel_id=1, replica_groups=mesh['mode'=4,'samp'=4,'pts'=2] {'mode','pts'}, use_global_device_ids=true, to_apply=%region_3.4 | all-reduce | flops 384 | bytes 3072 | tf_op jit(solution)/shard_map/psum | solution.py:221
  186.6 0.6 fusion.1
  187.2 6.3 %psum.30 = f32[]{:T(128)} all-reduce(f32[]{:T(128)} %fusion.1), channel_id=1, replica_groups=mesh['mode'=4,'samp'=4,'pts'=2] {'samp'}, use_global_device_ids=true, to_apply=%region_5.6 | all-reduce | flops 1 | bytes 8 | tf_op jit(solution)/shard_map/psum | solution.py:224
  194.1 0.6 multiply_reduce_fusion
  194.7 7.0 %psum.31 = f32[]{:T(128)} all-reduce(f32[]{:T(128)} %multiply_reduce_fusion), channel_id=1, replica_groups=mesh['mode'=4,'samp'=4,'pts'=2] {'samp'}, use_global_device_ids=true, to_apply=%region_7.8 | all-reduce | flops 1 | bytes 8 | tf_op jit(solution)/shard_map/psum | solution.py:226
  202.4 0.6 subtract_divide_fusion

commit v3 on v2

--- a/solution.py
+++ b/solution.py
@@ -13,10 +13,11 @@
 
 
 def kernel(
-    depth, chunks, coef_hbm, panel_hbm, mean_ref, load_ref, acc_ref,
-    coef, panel, out, core_in, cross_in, line_in_x, line_in_z,
+    depth, chunks, points, coef_hbm, panel_hbm, mean_ref, load_ref, result_ref,
+    acc_ref, parts, parts_in, diffs, diffs_in, coef, panel, out, core_in, cross_in, line_in_x, line_in_z,
     coef_send, coef_recv, coef_local, panel_sem,
     core_send, core_recv, cross_send, cross_recv, line_send, line_recv,
+    parts_send, parts_recv, diffs_send, diffs_recv,
 ):
     samp, line = lax.axis_index("samp"), lax.axis_index("mode")
     length = lax.axis_size("mode")
@@ -30,9 +31,14 @@
     barrier = pltpu.get_barrier_semaphore()
     for peer in peers:
         pl.semaphore_signal(barrier, inc=1, device_id={"samp": peer}, device_id_type=MESH)
-    for peer in (lax.rem(line + 1, length), lax.rem(line + last, length)):
-        pl.semaphore_signal(barrier, inc=1, device_id={"mode": peer}, device_id_type=MESH)
-    pl.semaphore_wait(barrier, 5)
+    side, sides = lax.axis_index("pts"), lax.axis_size("pts")
+    group = []
+    for on in range(length * sides):
+        if on > 0:
+            group.append((lax.rem(line + on // sides, length), lax.rem(side + on % sides, sides)))
+    for there, beside in group:
+        pl.semaphore_signal(barrier, inc=1, device_id={"mode": there, "pts": beside}, device_id_type=MESH)
+    pl.semaphore_wait(barrier, 3 + len(group))
 
     def panel_copy(j):
         slot = lax.rem(j, 2)
@@ -85,10 +91,10 @@
     def finish(j, field):
         columns = pl.ds(pl.multiple_of(j * WIDTH, WIDTH), WIDTH)
         weighted = load_ref[:, columns] * jnp.exp(field + mean_ref[:, columns])
-        total = acc_ref[...]
+        total = acc_ref[pl.ds(0, rows), :]
         for at in range(0, WIDTH, LANES):
             total = total + weighted[:, at : at + LANES]
-        acc_ref[...] = total
+        acc_ref[pl.ds(0, rows), :] = total
 
     def begin(j):
         @pl.when(j + 1 < chunks)
@@ -160,6 +166,70 @@
 
     lax.fori_loop(0, chunks + end, tick, 0)
 
+    per_lane = acc_ref[...].T
+    even = lax.rem(lax.broadcasted_iota(jnp.int32, per_lane.shape, 0), 2) == 0
+    fine_part = jnp.sum(per_lane, axis=0, keepdims=True)
+    coarse_part = jnp.sum(jnp.where(even, per_lane, 0.0), axis=0, keepdims=True)
+    sublane = lax.broadcasted_iota(jnp.int32, parts.shape, 0)
+    parts[...] = jnp.where(sublane == 0, fine_part, jnp.where(sublane == 1, coarse_part, 0.0))
+    is_end = (line == 0) | (line == last)
+    mine = (line // last) * sides + side
+
+    def parts_copy(i, slot):
+        there, beside = group[i]
+        return pltpu.make_async_remote_copy(
+            parts, parts_in.at[slot], parts_send.at[i], parts_recv.at[slot],
+            device_id={"mode": there, "pts": beside}, device_id_type=MESH,
+        )
+
+    @pl.when(is_end)
+    def _():
+        for i in range(len(group)):
+            parts_copy(i, mine).start()
+        parts_in[mine] = parts[...]
+
+    for slot in range(2 * sides):
+        @pl.when(jnp.logical_not(is_end & (mine == slot)))
+        def _(slot=slot):
+            parts_copy(0, slot).wait_recv()
+
+    total = parts_in[0]
+    for slot in range(1, 2 * sides):
+        total = total + parts_in[slot]
+    fine, coarse = total[0:1, :] / points, total[1:2, :] * (2.0 / points)
+    diffs[...] = jnp.broadcast_to(fine - coarse, diffs.shape)
+
+    def diffs_copy(i, slot):
+        return pltpu.make_async_remote_copy(
+            diffs, diffs_in.at[slot], diffs_send.at[i], diffs_recv.at[slot],
+            device_id={"samp": peers[i]}, device_id_type=MESH,
+        )
+
+    for i in range(3):
+        diffs_copy(i, samp).start()
+    diffs_in[samp] = diffs[...]
+    for slot in range(4):
+        @pl.when(samp != slot)
+        def _(slot=slot):
+            diffs_copy(0, slot).wait_recv()
+
+    inside = lax.broadcasted_iota(jnp.int32, (1, diffs.shape[1]), 1) < rows
+    level = [diffs_in[slot][0:1, :] for slot in range(4)]
+    summed = level[0] + level[1] + level[2] + level[3]
+    center = jnp.sum(jnp.where(inside, summed, 0.0), axis=1, keepdims=True) / (4 * rows)
+    squares = [jnp.where(inside, (one - center) * (one - center), 0.0) for one in level]
+    spread = jnp.sum(squares[0] + squares[1] + squares[2] + squares[3], axis=1, keepdims=True) / (4 * rows)
+    standardized = (diffs[0:1, :] - center) / jnp.sqrt(spread + 1e-06)
+    result_ref[...] = standardized[:, 0:rows]
+
+    for i in range(3):
+        diffs_copy(i, samp).wait_send()
+
+    @pl.when(is_end)
+    def _():
+        for i in range(len(group)):
+            parts_copy(i, mine).wait_send()
+
     def drain(j, carry):
         core_copy(j).wait_send()
         even, final = lax.rem(j, 2) == 0, place(j) == last
@@ -184,20 +254,27 @@
 CROSS_LAG, LINE_LAG, WIDE_LAG = 3, 2, 4
 
 
-def lane_sums(coefficients, panels, mean_field, load):
+def lined(points, coefficients, panels, mean_field, load):
     rows = coefficients.shape[0]
-    depth, points = panels.shape
-    chunks = points // WIDTH
+    depth, own = panels.shape
+    chunks = own // WIDTH
     every = pl.BlockSpec(memory_space=pl.ANY)
     here = pl.BlockSpec(memory_space=pltpu.VMEM)
     dma = pltpu.SemaphoreType.DMA
     f32 = jnp.float32
-    return pl.pallas_call(
-        functools.partial(kernel, depth, chunks),
-        out_shape=jax.ShapeDtypeStruct((rows, LANES), f32),
+    length, sides = lax.axis_size("mode"), lax.axis_size("pts")
+    padded = pl.cdiv(rows, LANES) * LANES
+    result = pl.pallas_call(
+        functools.partial(kernel, depth, chunks, points),
+        out_shape=jax.ShapeDtypeStruct((1, rows), f32),
         in_specs=[every, every, here, here],
         out_specs=here,
         scratch_shapes=[
+            pltpu.VMEM((padded, LANES), f32),
+            pltpu.VMEM((8, padded), f32),
+            pltpu.VMEM((2 * sides, 8, padded), f32),
+            pltpu.VMEM((8, padded), f32),
+            pltpu.VMEM((4, 8, padded), f32),
             pltpu.VMEM((4 * rows, depth), jnp.bfloat16),
             pltpu.VMEM((2, depth, WIDTH), jnp.bfloat16),
             pltpu.VMEM((chunks, 4 * rows, WIDTH), f32),
@@ -207,24 +284,13 @@
             pltpu.VMEM((chunks // 2, 2 * rows, WIDTH), f32),
             dma((3,)), dma((3,)), dma, dma((2,)),
             dma((chunks,)), dma((chunks,)), dma((chunks,)), dma((chunks,)), dma((chunks,)), dma((chunks,)),
+            dma((length * sides - 1,)), dma((2 * sides,)), dma((3,)), dma((4,)),
         ],
         compiler_params=pltpu.CompilerParams(
             collective_id=0, has_side_effects=True, vmem_limit_bytes=67043328
         ),
     )(coefficients, panels, mean_field[None, :], load[None, :])
-
-
-def lined(points, coefficients, panels, mean_field, load):
-    sums = lane_sums(coefficients, panels, mean_field, load)
-    even = (lax.broadcasted_iota(jnp.int32, (1, LANES), 1) % 2) == 0
-    parts = jnp.sum(sums, axis=1), jnp.sum(jnp.where(even, sums, 0.0), axis=1)
-    fine, coarse = lax.psum(parts, ("mode", "pts"))
-    level_diff = fine / points - coarse * (2.0 / points)
-    total = level_diff.shape[0] * lax.axis_size("samp")
-    center = lax.psum(jnp.sum(level_diff), "samp") / total
-    shifted = level_diff - center
-    spread = lax.psum(jnp.sum(shifted * shifted), "samp") / total
-    return shifted / jnp.sqrt(spread + 1e-06)
+    return result[0]
 
 
 def gathered(points, coefficients, panels, mean_field, load):

time: 204 us -> 175 us (0.86)
  blocking collectives: 38.4 us -> 0 us
  Pallas kernels: 160 us -> 173 us
  other arithmetic: 3.34 us -> 0 us
    psum x3 -> x0, blocking collectives: 38.4 us -> none  [the longest x1 25.2 us: lined(): fine, coarse = lax.psum(parts, ('mode', 'pts'))]
    pallas_call x1, Pallas kernels: 160 us -> 173 us  [lined(): pl.pallas_call(functools.partial(kernel, depth, chunks, points), out_shap...]
    reduce_sum x3 -> x0, other arithmetic: 2.25 us -> none  [the longest x1 1.04 us: lined(): parts = (jnp.sum(sums, axis=1), jnp.sum(jnp.where(even, sums, 0.0), axis=1))]
where the time goes in v3:
time: 175 us; the launch traced here: 174 us
  Pallas kernels  173 us (99%)
    pallas_call x1, Pallas kernels, lined(): pl.pallas_call(functools.partial(kernel, depth, chunks, points), out_shap...  173 us

profile of v3, /device:TPU:0, one launch (start us, length us, event | category | flops | bytes accessed | tf_op | source)
XLA Modules:
  0.0 174.0 jit_solution(8349382675188038098)
XLA Ops:
  0.0 172.8 %shard_map.46 = f32[1,192]{1,0:T(1,128)} custom-call(bf16[192,3072]{1,0:T(8,128)(2,1)} %coef_hbm.1, bf16[768,8192]{1,0:T(8,128)(2,1)} %panel_hbm.1, f32[1,8192]{1,0:T(1,128)} %bitcast.3, f32[1,8192]{1,0:T(1,128)} %bitcast.4), custom_call_target="tpu_custom_call" | custom-call | tf_op jit(solution)/shard_map/pallas_call | solution.py:267
  172.8 1.2 copy.6

commit v4 on v3

--- a/solution.py
+++ b/solution.py
@@ -8,16 +8,18 @@
 from jax.sharding import PartitionSpec as P
 
 MESH = pl.DeviceIdType.MESH
-WIDTH = 256
+WIDTH = 128
+PERIOD, WIDE = 2, 1
+TAIL = 4
 LANES = 128
 
 
 def kernel(
     depth, chunks, points, coef_hbm, panel_hbm, mean_ref, load_ref, result_ref,
-    acc_ref, parts, parts_in, diffs, diffs_in, coef, panel, out, core_in, cross_in, line_in_x, line_in_z,
+    acc_ref, parts, parts_in, diffs, diffs_in, coef, panel, out, core_in, cross_in, line_in,
     coef_send, coef_recv, coef_local, panel_sem,
     core_send, core_recv, cross_send, cross_recv, line_send, line_recv,
-    parts_send, parts_recv, diffs_send, diffs_recv,
+    parts_send, parts_recv, diffs_send, diffs_recv, relay_send, relay_recv,
 ):
     samp, line = lax.axis_index("samp"), lax.axis_index("mode")
     length = lax.axis_size("mode")
@@ -45,11 +47,22 @@
         columns = pl.ds(pl.multiple_of(j * WIDTH, WIDTH), WIDTH)
         return pltpu.make_async_copy(panel_hbm.at[:, columns], panel.at[slot], panel_sem.at[slot])
 
+    half = rows // 2
+    mine_half = pl.multiple_of(side * half, half)
+
     def coef_copy(i):
         columns = pl.ds(pl.multiple_of(peers[i] * depth, depth), depth)
-        return pltpu.make_async_remote_copy(
-            coef_hbm.at[:, columns], coef.at[pl.ds((i + 1) * rows, rows), :],
+        first, count = (0, rows) if i == 1 else (mine_half, half)
+        return pltpu.make_async_remote_copy(
+            coef_hbm.at[pl.ds(first, count), columns], coef.at[pl.ds((i + 1) * rows + first, count), :],
             coef_send.at[i], coef_recv.at[i], device_id={"samp": peers[i]}, device_id_type=MESH,
+        )
+
+    def coef_relay(i):
+        block = coef.at[pl.ds((i + 1) * rows + mine_half, half), :]
+        return pltpu.make_async_remote_copy(
+            block, block, relay_send.at[i // 2], relay_recv.at[i // 2],
+            device_id={"pts": 1 - side}, device_id_type=MESH,
         )
 
     for i in (0, 2, 1):
@@ -74,17 +87,19 @@
         )
 
     def up(j):
-        return lax.rem(j // 2, 2)
+        return lax.rem(j // PERIOD, 2)
+
+    def is_wide(j):
+        return (lax.rem(j, PERIOD) >= PERIOD - WIDE) & (j < chunks - TAIL)
 
     def place(j):
         return up(j) * line + (1 - up(j)) * (last - line)
 
     def line_copy(j, kind):
         size = (1 + kind) * rows
-        into = line_in_z if kind else line_in_x
         target = lax.rem(line + 2 * up(j) - 1 + length, length)
         return pltpu.make_async_remote_copy(
-            out.at[j, pl.ds(0, size), :], into.at[j // 2],
+            out.at[j, pl.ds(0, size), :], line_in.at[j, pl.ds(0, size), :],
             line_send.at[j], line_recv.at[j], device_id={"mode": target}, device_id_type=MESH,
         )
 
@@ -109,11 +124,11 @@
         core_copy(j).wait_recv()
         out[j, pl.ds(0, 2 * rows), :] += core_in[j]
 
-        @pl.when(lax.rem(j, 2) == 0)
+        @pl.when(jnp.logical_not(is_wide(j)))
         def _():
             cross_copy(j).start()
 
-        @pl.when((lax.rem(j, 2) == 1) & (place(j) == 0))
+        @pl.when(is_wide(j) & (place(j) == 0))
         def _():
             line_copy(j, 1).start()
 
@@ -130,13 +145,13 @@
         def _():
             line_copy(j, kind).wait_recv()
             if at < last:
-                out[j, pl.ds(0, (1 + kind) * rows), :] += (line_in_z if kind else line_in_x)[j // 2]
+                out[j, pl.ds(0, (1 + kind) * rows), :] += line_in[j, pl.ds(0, (1 + kind) * rows), :]
                 line_copy(j, kind).start()
             elif kind:
-                out[j, pl.ds(0, 2 * rows), :] += line_in_z[j // 2]
+                out[j, pl.ds(0, 2 * rows), :] += line_in[j]
                 cross_copy(j).start()
             else:
-                finish(j, out[j, pl.ds(0, rows), :] + line_in_x[j // 2])
+                finish(j, out[j, pl.ds(0, rows), :] + line_in[j, pl.ds(0, rows), :])
 
     def back(j):
         @pl.when(place(j) == last)
@@ -145,14 +160,18 @@
             finish(j, out[j, pl.ds(0, rows), :] + cross_in[j])
 
     own.wait()
-    for i in range(3):
-        coef_copy(i).wait()
-
-    stages = [(0, None, begin), (1, None, joined), (1 + CROSS_LAG, 0, crossed)]
+    for i in (0, 2):
+        coef_copy(i).wait_recv()
+        coef_relay(i).start()
+    coef_copy(1).wait_recv()
+    for i in (0, 2):
+        coef_relay(i).wait_recv()
+
+    stages = [(0, None, begin), (JOIN_LAG, None, joined), (JOIN_LAG + CROSS_LAG, 0, crossed)]
     for at in range(1, last + 1):
-        stages.append((1 + CROSS_LAG + LINE_LAG * at, 0, functools.partial(hop, kind=0, at=at)))
-        stages.append((1 + WIDE_LAG * at, 1, functools.partial(hop, kind=1, at=at)))
-    stages.append((1 + WIDE_LAG * last + CROSS_LAG, 1, back))
+        stages.append((JOIN_LAG + CROSS_LAG + LINE_LAG * at, 0, functools.partial(hop, kind=0, at=at)))
+        stages.append((JOIN_LAG + WIDE_LAG * at, 1, functools.partial(hop, kind=1, at=at)))
+    stages.append((JOIN_LAG + WIDE_LAG * last + CROSS_LAG, 1, back))
     end = max(lag for lag, _, _ in stages)
 
     def tick(t, carry):
@@ -160,7 +179,8 @@
             j = t - lag
             here = (j >= 0) & (j < chunks)
             if kind is not None:
-                here = here & (lax.rem(j + 2 * end, 2) == kind)
+                wide = is_wide(j)
+                here = here & (wide if kind else jnp.logical_not(wide))
             pl.when(here)(functools.partial(stage, j))
         return carry
 
@@ -223,7 +243,10 @@
     result_ref[...] = standardized[:, 0:rows]
 
     for i in range(3):
+        coef_copy(i).wait_send()
         diffs_copy(i, samp).wait_send()
+    for i in (0, 2):
+        coef_relay(i).wait_send()
 
     @pl.when(is_end)
     def _():
@@ -232,17 +255,17 @@
 
     def drain(j, carry):
         core_copy(j).wait_send()
-        even, final = lax.rem(j, 2) == 0, place(j) == last
-
-        @pl.when(even | final)
+        wide, final = is_wide(j), place(j) == last
+
+        @pl.when(jnp.logical_not(wide) | final)
         def _():
             cross_copy(j).wait_send()
 
-        @pl.when(even & (place(j) < last))
+        @pl.when(jnp.logical_not(wide) & (place(j) < last))
         def _():
             line_copy(j, 0).wait_send()
 
-        @pl.when((lax.rem(j, 2) == 1) & (place(j) < last))
+        @pl.when(wide & (place(j) < last))
         def _():
             line_copy(j, 1).wait_send()
 
@@ -251,7 +274,7 @@
     lax.fori_loop(0, chunks, drain, 0)
 
 
-CROSS_LAG, LINE_LAG, WIDE_LAG = 3, 2, 4
+JOIN_LAG, CROSS_LAG, LINE_LAG, WIDE_LAG = 2, 4, 3, 5
 
 
 def lined(points, coefficients, panels, mean_field, load):
@@ -280,11 +303,10 @@
             pltpu.VMEM((chunks, 4 * rows, WIDTH), f32),
             pltpu.VMEM((chunks, 2 * rows, WIDTH), f32),
             pltpu.VMEM((chunks, rows, WIDTH), f32),
-            pltpu.VMEM((chunks // 2, rows, WIDTH), f32),
-            pltpu.VMEM((chunks // 2, 2 * rows, WIDTH), f32),
+            pltpu.VMEM((chunks, 2 * rows, WIDTH), f32),
             dma((3,)), dma((3,)), dma, dma((2,)),
             dma((chunks,)), dma((chunks,)), dma((chunks,)), dma((chunks,)), dma((chunks,)), dma((chunks,)),
-            dma((length * sides - 1,)), dma((2 * sides,)), dma((3,)), dma((4,)),
+            dma((length * sides - 1,)), dma((2 * sides,)), dma((3,)), dma((4,)), dma((2,)), dma((2,)),
         ],
         compiler_params=pltpu.CompilerParams(
             collective_id=0, has_side_effects=True, vmem_limit_bytes=67043328
@@ -322,7 +344,7 @@
 
     def run(coefficients, panels, mean_field, load):
         def inner(*args):
-            form = lined if mesh.shape["samp"] == 4 and mesh.shape["mode"] > 2 else gathered
+            form = lined if mesh.shape["samp"] == 4 and mesh.shape["pts"] == 2 and mesh.shape["mode"] > 2 else gathered
             return form(mean_field.shape[0], *args)
 
         return jax.shard_map(inner, mesh=mesh, in_specs=in_specs, out_specs=P("samp"), check_vma=False)(

time: 175 us -> 154 us (0.88)
  Pallas kernels: 173 us -> 152 us
    pallas_call x1, Pallas kernels: 173 us -> 152 us  [lined(): pl.pallas_call(functools.partial(kernel, depth, chunks, points), out_shap...]
where the time goes in v4:
time: 154 us; the launch traced here: 153 us
  Pallas kernels  152 us (99%)
    pallas_call x1, Pallas kernels, lined(): pl.pallas_call(functools.partial(kernel, depth, chunks, points), out_shap...  152 us

profile of v4, /device:TPU:0, one launch (start us, length us, event | category | flops | bytes accessed | tf_op | source)
XLA Modules:
  0.0 153.4 jit_solution(2068106271612440675)
XLA Ops:
  0.0 152.2 %shard_map.46 = f32[1,192]{1,0:T(1,128)} custom-call(bf16[192,3072]{1,0:T(8,128)(2,1)} %coef_hbm.1, bf16[768,8192]{1,0:T(8,128)(2,1)} %panel_hbm.1, f32[1,8192]{1,0:T(1,128)} %bitcast.3, f32[1,8192]{1,0:T(1,128)} %bitcast.4), custom_call_target="tpu_custom_call" | custom-call | tf_op jit(solution)/shard_map/pallas_call | solution.py:290
  152.2 1.2 copy.6

commit v5 on v4

--- a/solution.py
+++ b/solution.py
@@ -10,7 +10,7 @@
 MESH = pl.DeviceIdType.MESH
 WIDTH = 128
 PERIOD, WIDE = 2, 1
-TAIL = 4
+TAIL = 8
 LANES = 128
 
 

time: 154 us -> 156 us (1.013)
  no operation moved by 1% of the time
where the time goes in v5:
time: 156 us; the launch traced here: 155 us
  Pallas kernels  153 us (98%)
    pallas_call x1, Pallas kernels, lined(): pl.pallas_call(functools.partial(kernel, depth, chunks, points), out_shap...  153 us

profile of v5, /device:TPU:0, one launch (start us, length us, event | category | flops | bytes accessed | tf_op | source)
XLA Modules:
  0.0 154.7 jit_solution(16501106562219464951)
XLA Ops:
  0.0 153.4 %shard_map.46 = f32[1,192]{1,0:T(1,128)} custom-call(bf16[192,3072]{1,0:T(8,128)(2,1)} %coef_hbm.1, bf16[768,8192]{1,0:T(8,128)(2,1)} %panel_hbm.1, f32[1,8192]{1,0:T(1,128)} %bitcast.3, f32[1,8192]{1,0:T(1,128)} %bitcast.4), custom_call_target="tpu_custom_call" | custom-call | tf_op jit(solution)/shard_map/pallas_call | solution.py:290
  153.4 1.2 copy.6
